TPU v7x, 32 devices: a whole 2x2x4 slice. The times are simulated.
32 devices in a mesh: groups: 2 (over x), seq: 16 (over z, y, core).
Axes of the slice: x: 2, y: 2, z: 4, core: 2. Of those that a mesh axis runs over, the one named last changes fastest.
Arguments:
- residual: float32 [4, 16, 128, 1152], P('groups', 'seq'), parts along dimension 0, may hold values from -16 to 16
- w_qkv: bfloat16 [1152, 3456], replicated, may hold values from -0.15 to 0.15
- w_proj: bfloat16 [1152, 1152], replicated, may hold values from -0.1875 to 0.1875
- q_gain: float32 [1152], replicated, may hold values from 0.5 to 7
- k_gain: float32 [1152], replicated, may hold values from 0.5 to 7
- step_mods: float32 [30, 3, 1152], replicated, may hold values from -4 to 4
- timestep: int32 [2], P('groups'), parts along dimension 0, may hold values from 0 to 29, as said below
Outputs:
- updated: float32 [4, 16, 128, 1152], P('groups', 'seq'), parts along dimension 0
There are 2 independent parts, one for each index of `groups`. A program takes and returns all parts, laid end to end along the dimension named above; an argument that names none is the same for every part. Nothing has to cross between parts.
Inputs may be any that keep to these rules, and one draw needn't show every extreme that they name: `timestep`: the first part takes a step from the first half of the table, the second part the last step.
All inputs are finite; a program needn't handle non-finite values.
Results may differ from a plain program's by a relative error of at most 0.002.
Values may be sent and summed in bfloat16 or wider, within the bound.
No kernel may reach another device: no remote copies, remote signals or barrier semaphores. Data moves between devices by JAX's collectives and lax.ppermute only.
A program may use at most 64 MiB of HBM per device.

v0:
```python
import jax
import jax.numpy as jnp
from jax import lax
from jax.sharding import PartitionSpec as P

HEADS = 16
HEAD_DIM = 72


def layer_modulate(rows, shift_row, scale_row):
    centre = jnp.mean(rows, axis=-1, keepdims=True)
    centred = rows - centre
    variance = jnp.mean(centred * centred, axis=-1, keepdims=True)
    return (centred * lax.rsqrt(variance + 1e-06) * (1.0 + scale_row) + shift_row).astype(
        jnp.bfloat16
    )


def head_norm(vectors, gain):
    square = jnp.mean(vectors * vectors, axis=-1, keepdims=True)
    return (vectors * lax.rsqrt(square + 1e-06) * gain).astype(jnp.bfloat16)


def temporal_heads(modulated, w_qkv, q_gain, k_gain):
    branch, frames, patches, width = modulated.shape
    projected = jnp.dot(modulated.reshape(-1, width), w_qkv, preferred_element_type=jnp.float32)
    projected = projected.reshape(branch, frames, patches, 3, HEADS, HEAD_DIM)
    queries = head_norm(projected[:, :, :, 0], q_gain.reshape(HEADS, HEAD_DIM))
    key_vecs = head_norm(projected[:, :, :, 1], k_gain.reshape(HEADS, HEAD_DIM))
    values = projected[:, :, :, 2].astype(jnp.bfloat16)
    block_rows = min(frames, 512)
    block_count = frames // block_rows
    query_blocks = jnp.moveaxis(
        queries.reshape(branch, block_count, block_rows, patches, HEADS, HEAD_DIM), 1, 0
    )

    def one_block(query_part):
        scores = jnp.einsum(
            "bqphd,bkphd->bphqk", query_part, key_vecs, preferred_element_type=jnp.float32
        ) * HEAD_DIM ** (-0.5)
        top = jnp.max(scores, axis=-1, keepdims=True)
        weights = jnp.exp(scores - top)
        total = jnp.sum(weights, axis=-1, keepdims=True)
        probs = (weights / total).astype(jnp.bfloat16)
        mixed = jnp.einsum("bphqk,bkphd->bqphd", probs, values, preferred_element_type=jnp.float32)
        return mixed.astype(jnp.bfloat16)

    attended = jnp.moveaxis(lax.map(one_block, query_blocks), 0, 1)
    return attended.reshape(branch, frames, patches, width)


def body(residual, w_qkv, w_proj, q_gain, k_gain, step_mods, timestep):
    modulation = lax.dynamic_index_in_dim(step_mods, timestep[0], 0, keepdims=False)
    shift_row = modulation[0]
    scale_row = modulation[1]
    gate_row = modulation[2]
    width = residual.shape[-1]
    modulated = layer_modulate(residual, shift_row, scale_row)
    attended = lax.all_to_all(
        temporal_heads(
            lax.all_to_all(modulated, "seq", split_axis=2, concat_axis=1, tiled=True),
            w_qkv,
            q_gain,
            k_gain,
        ),
        "seq",
        split_axis=1,
        concat_axis=2,
        tiled=True,
    )
    output = jnp.dot(attended.reshape(-1, width), w_proj, preferred_element_type=jnp.float32)
    return residual + gate_row * output.reshape(attended.shape)


def solution(mesh):
    in_specs = (P("groups", "seq", None, None), P(), P(), P(), P(), P(), P("groups"))
    out_specs = P("groups", "seq", None, None)
    return jax.shard_map(body, mesh=mesh, in_specs=in_specs, out_specs=out_specs, check_vma=False)
```

profile of v0, /device:TPU:0, one launch (start us, length us, event | category | flops | bytes accessed | tf_op | source)
XLA Modules:
  0.0 79.1 jit_solution(4661231158813859718)
XLA Ops:
  0.8 1.4 %reduce_sum.46 = f32[2,128]{1,0:T(2,128)S(1)} reduce(f32[2,1,128,1152]{3,2,1,0:T(8,128)} %param.7, f32[]{:T(128)} %constant.18.clone.1), dimensions={1,3}, to_apply=%region_0.1 | reduce | flops 294656 | bytes 1180676 | tf_op jit(solution)/shard_map/reduce_sum | solution.py:11
  2.2 1.5 %multiply_reduce_fusion.3 = f32[2,128]{1,0:T(2,128)S(1)} fusion(f32[2,1,128,1152]{3,2,1,0:T(8,128)} %param.7, f32[2,128]{1,0:T(2,128)S(1)} %broadcast_multiply_fusion), kind=kLoop, calls=%fused_computation.20 | loop fusion | flops 884480 | bytes 1181696 | tf_op jit(solution)/shard_map/reduce_sum | solution.py:13
  3.8 0.9 %dynamic-slice_reduce_fusion.1 = (f32[1152]{0:T(1024)S(1)}, f32[1152]{0:T(1024)S(1)}, f32[1152]{0:T(1024)S(1)}) fusion(f32[30,3,1152]{2,0,1:T(8,128)} %param.12, s32[]{:T(128)S(6)} %select_n.4, s32[]{:T(128)S(6)} %add.74, s32[]{:T(128)S(6)} %add.75), kind=kLoop, calls=%fused_computation.38 | loop fusion | flops 1152 | bytes 27660 | tf_op jit(solution)/shard_map/slice | solution.py:56
  4.6 1.5 %add_convert_fusion = bf16[2,1,128,1152]{3,2,1,0:T(8,128)(2,1)S(1)} fusion(f32[2,1,128,1152]{3,2,1,0:T(8,128)} %param.7, f32[1152]{0:T(1024)S(1)} %get-tuple-element.24, f32[1152]{0:T(1024)S(1)} %get-tuple-element.22, f32[2,128]{1,0:T(2,128)S(1)} %add_rsqrt_fusion.2, f32[2,128]{1,0:T(2,128)S(1)} %broadcast_multiply_fusion), kind=kLoop, calls=%fused_computation.19 | loop fusion | flops 1474560 | bytes 1780736 | tf_op jit(solution)/shard_map/convert_element_type | solution.py:14
  6.2 1.4 %copy.66 = bf16[2,1,128,1152]{3,0,1,2:T(2,128)(2,1)} copy(bf16[2,1,128,1152]{3,2,1,0:T(8,128)(2,1)S(1)} %add_convert_fusion) | data formatting | bytes 1179648 | tf_op jit(solution)/shard_map/convert_element_type | solution.py:14
  7.6 7.4 %all-to-all-start = ((bf16[2,1,128,1152]{3,0,1,2:T(2,128)(2,1)}), bf16[2,1,128,1152]{3,0,1,2:T(2,128)(2,1)S(1)}, u32[]{:S(2)}, u32[]{:S(2)}) async-start(bf16[2,1,128,1152]{3,0,1,2:T(2,128)(2,1)} %copy.66), calls=%async_computation | async-start | bytes 1179648 | tf_op jit(solution)/shard_map/all_to_all | solution.py:61
  15.0 0.0 copy-start.1
  15.0 0.0 copy-start.2
  15.1 11.5 %copy.68 = bf16[1152,3456]{0,1:T(8,128)(2,1)} copy(bf16[1152,3456]{1,0:T(8,128)(2,1)} %param.8) | data formatting | bytes 15925248 | tf_op args[1]
  26.6 0.1 mul.88
  26.7 0.0 copy-done.2
  26.7 0.1 mul.94
  26.8 3.7 %all-to-all-done = bf16[2,1,128,1152]{3,0,1,2:T(2,128)(2,1)S(1)} async-done(((bf16[2,1,128,1152]{3,0,1,2:T(2,128)(2,1)}), bf16[2,1,128,1152]{3,0,1,2:T(2,128)(2,1)S(1)}, u32[]{:S(2)}, u32[]{:S(2)}) %all-to-all-start) | async-done | bytes 589856 | tf_op jit(solution)/shard_map/all_to_all | solution.py:61
  30.4 6.6 %fusion.14 = f32[2,16,8,3,16,72]{5,2,4,3,1,0:T(8,128)S(1)} fusion(bf16[3,16,72,1152,1,1]{3,2,1,0,5,4:T(8,128)(2,1)} %bitcast.55, bf16[2,1,128,1152]{3,0,1,2:T(2,128)(2,1)S(1)} %all-to-all-done), kind=kOutput, calls=%fused_computation.28 | convolution fusion | flops 2038431744 | bytes 12091392 | tf_op jit(solution)/shard_map/dot_general | solution.py:26
  37.0 1.2 %multiply_reduce_fusion.1 = (f32[2,16,8,16]{2,3,1,0:T(8,128)S(1)}, f32[2,16,8,16]{2,3,1,0:T(8,128)S(1)}) fusion(f32[2,16,8,3,16,72]{5,2,4,3,1,0:T(8,128)S(1)} %fusion.14), kind=kLoop, calls=%fused_computation.14 | loop fusion | flops 1171456 | bytes 2392064 | tf_op jit(solution)/shard_map/reduce_sum | solution.py:20
  38.2 1.1 %fusion.7 = bf16[2,16,8,16,72]{4,2,3,1,0:T(8,128)(2,1)} fusion(f32[2,16,8,3,16,72]{5,2,4,3,1,0:T(8,128)S(1)} %fusion.14), kind=kLoop, calls=%fused_computation.21 | loop fusion | bytes 1179648 | tf_op jit(solution)/shard_map/convert_element_type | solution.py:30
  39.3 0.1 add_rsqrt_fusion
  39.4 2.3 %multiply_convert_fusion.1 = (bf16[2,16,8,16,72]{4,2,3,1,0:T(8,128)(2,1)}, bf16[2,16,8,16,72]{4,2,3,1,0:T(8,128)(2,1)}) fusion(f32[2,16,8,3,16,72]{5,2,4,3,1,0:T(8,128)S(1)} %fusion.14, f32[16,72]{1,0:T(8,128)S(1)} %mul.88, f32[2,16,8,16]{2,3,1,0:T(8,128)S(1)} %get-tuple-element.30, f32[16,72]{1,0:T(8,128)S(1)} %mul.94, ...), kind=kLoop, calls=%fused_computation.13 | loop fusion | flops 1769472 | bytes 3580928 | tf_op jit(solution)/shard_map/convert_element_type | solution.py:21
  41.7 5.8 %fusion.33 = (f32[2,8,16,16]{3,2,1,0:T(8,128)S(1)}, f32[2,8,16,16,16]{3,4,2,1,0:T(8,128)}) fusion(bf16[2,16,8,16,72]{4,2,3,1,0:T(8,128)(2,1)} %get-tuple-element.26, bf16[2,16,8,16,72]{4,2,3,1,0:T(8,128)(2,1)} %get-tuple-element.25), kind=kOutput, calls=%fused_computation.42 | convolution fusion | flops 9633807 | bytes 1458176 | tf_op jit(solution)/shard_map/while/body/eval_jaxpr/sub | solution.py:42
  47.5 3.3 %fusion.6 = bf16[2,16,8,16,72]{4,1,3,2,0:T(8,128)(2,1)S(1)} fusion(f32[2,8,16,16,16]{3,4,2,1,0:T(8,128)} %get-tuple-element.28, bf16[2,16,8,16,72]{4,2,3,1,0:T(8,128)(2,1)} %fusion.7, f32[2,8,16,16]{3,2,1,0:T(8,128)S(1)} %get-tuple-element.27), kind=kOutput, calls=%fused_computation.18 | convolution fusion | flops 9863168 | bytes 1458176 | tf_op jit(solution)/shard_map/while/body/eval_jaxpr/bphqk,bkphd->bqphd/dot_general | solution.py:45
  50.8 1.2 %copy.81 = bf16[2,16,8,16,72]{4,3,2,0,1:T(8,128)(2,1)} copy(bf16[2,16,8,16,72]{4,1,3,2,0:T(8,128)(2,1)S(1)} %fusion.6) | data formatting | bytes 1179648 | tf_op jit(solution)/shard_map/reshape;transpose | solution.py:49
  52.0 2.2 %reshape.89 = bf16[2,16,8,1152]{3,2,0,1:T(8,128)(2,1)S(1)} reshape(bf16[2,16,8,16,72]{4,3,2,0,1:T(8,128)(2,1)} %copy.81) | data formatting | bytes 1179648 | tf_op jit(solution)/shard_map/reshape;transpose | solution.py:49
  54.3 21.5 %all_to_all.8 = bf16[2,16,8,1152]{3,2,0,1:T(8,128)(2,1)S(1)} all-to-all(bf16[2,16,8,1152]{3,2,0,1:T(8,128)(2,1)S(1)} %reshape.89), channel_id=1, replica_groups=mesh['groups'=2,'seq'=16] {'seq'}, dimensions={1} | all-to-all | bytes 1179648 | tf_op jit(solution)/shard_map/all_to_all | solution.py:59
  75.8 3.3 %fusion.3 = f32[2,1,128,1152]{3,2,1,0:T(8,128)} fusion(bf16[1152,1152]{1,0:T(8,128)(2,1)S(1)} %copy-done, f32[2,1,128,1152]{3,2,1,0:T(8,128)} %param.7, bf16[2,16,8,1152]{3,2,0,1:T(8,128)(2,1)S(1)} %all_to_all.8, f32[1152]{0:T(1024)S(1)} %get-tuple-element.20), kind=kOutput, calls=%fused_computation.4 | convolution fusion | flops 680067072 | bytes 5607936 | tf_op jit(solution)/shard_map/dot_general | solution.py:71
  (5 shorter events, 0.0 us)
Async XLA Ops:
  0.0 75.8 %copy-start = (bf16[1152,1152]{1,0:T(8,128)(2,1)S(1)}, bf16[1152,1152]{1,0:T(8,128)(2,1)}, u32[]{:S(2)}) copy-start(bf16[1152,1152]{1,0:T(8,128)(2,1)} %param.9) | copy-start | bytes 7962628
  7.6 22.8 %all-to-all-start = ((bf16[2,1,128,1152]{3,0,1,2:T(2,128)(2,1)}), bf16[2,1,128,1152]{3,0,1,2:T(2,128)(2,1)S(1)}, u32[]{:S(2)}, u32[]{:S(2)}) async-start(bf16[2,1,128,1152]{3,0,1,2:T(2,128)(2,1)} %copy.66), calls=%async_computation | async-start | bytes 1179648 | tf_op jit(solution)/shard_map/all_to_all | solution.py:61
  15.0 11.5 %copy-start.1 = (f32[1152]{0:T(1024)S(1)}, f32[1152]{0:T(1024)}, u32[]{:S(2)}) copy-start(f32[1152]{0:T(1024)} %param.10) | copy-start | bytes 13828
  15.0 11.6 %copy-start.2 = (f32[1152]{0:T(1024)S(1)}, f32[1152]{0:T(1024)}, u32[]{:S(2)}) copy-start(f32[1152]{0:T(1024)} %param.11) | copy-start | bytes 13828
where the time goes:
time: 79.8 us; the launch traced here: 79.1 us
  blocking collectives  21.5 us (27%)
  matrix products  19 us (24%)
  local copies, waits for them, and re-layouts  17.7 us (22%)
  other arithmetic  8.88 us (11%)
  starting transfers between devices  7.41 us (9%)
  waiting for transfers between devices  3.65 us (5%)
  between operations  0.91 us (1%)
    all_to_all x1, blocking collectives, body(): lax.all_to_all(temporal_heads(lax.all_to_all(modulated, 'seq', split_axis...  21.5 us
    unnamed x7, local copies, waits for them, and re-layouts  11.5 us
    all_to_all x1, starting transfers between devices, body(): lax.all_to_all(modulated, 'seq', split_axis=2, concat_axis=1, tiled=True)  7.41 us
    dot_general x1, matrix products, temporal_heads(): jnp.dot(modulated.reshape(-1, width), w_qkv, preferred_element_type=jnp.f...  6.59 us
    sub x1, matrix products, one_block(): weights = jnp.exp(scores - top)  5.79 us
    all_to_all x1, waiting for transfers between devices, body(): lax.all_to_all(modulated, 'seq', split_axis=2, concat_axis=1, tiled=True)  3.65 us
    another operation x2, local copies, waits for them, and re-layouts, temporal_heads(): return attended.reshape(branch, frames, patches, width)  3.48 us
    dot_general x1, matrix products, body(): jnp.dot(attended.reshape(-1, width), w_proj, preferred_element_type=jnp.f...  3.31 us
  transfers between devices with their start and end apart: 1, of which 1 were waited for; matrix products, arithmetic and copies ran while one was open for 15% of the time, Pallas kernels for 0%

commit v1 on v0

v1 whole, which is shorter than its diff:
```python
import functools

import jax
import jax.numpy as jnp
from jax import lax
from jax.experimental import pallas as pl
from jax.experimental.pallas import tpu as pltpu
from jax.sharding import PartitionSpec as P

HEADS = 16
HEAD_DIM = 72
LANES = 128
F32 = jnp.float32
BF16 = jnp.bfloat16
VMEM = pltpu.VMEM


def modulate_kernel(step_ref, rows_ref, mods_ref, out_ref):
    del step_ref
    rows = rows_ref[0]
    shift_row, scale_row = mods_ref[0, 0:1, :], mods_ref[0, 1:2, :]
    centre = jnp.mean(rows, axis=-1, keepdims=True)
    centred = rows - centre
    variance = jnp.mean(centred * centred, axis=-1, keepdims=True)
    normed = centred * lax.rsqrt(variance + 1e-06) * (1.0 + scale_row) + shift_row
    out_ref[:, 0] = normed.reshape(out_ref.shape[0], *out_ref.shape[2:]).astype(BF16)


def modulate(rows, step_mods, timestep, n):
    branch, patches, width = rows.shape
    share = patches // n
    return pl.pallas_call(
        modulate_kernel,
        out_shape=jax.ShapeDtypeStruct((n, branch, share, width), BF16),
        grid_spec=pltpu.PrefetchScalarGridSpec(
            num_scalar_prefetch=1,
            grid=(branch,),
            in_specs=[
                pl.BlockSpec((1, patches, width), lambda b, step: (b, 0, 0)),
                pl.BlockSpec((1, 3, width), lambda b, step: (step[0], 0, 0)),
            ],
            out_specs=pl.BlockSpec((n, 1, share, width), lambda b, step: (0, b, 0, 0)),
        ),
        name="modulate",
    )(timestep, rows, step_mods)


def split_dot(wide, ones):
    high = wide.astype(BF16)
    low = (wide - high.astype(F32)).astype(BF16)
    return jnp.dot(high, ones, preferred_element_type=F32) + jnp.dot(
        low, ones, preferred_element_type=F32
    )


def head_of(shape, feature_dim, head_dim):
    feature = lax.broadcasted_iota(jnp.int32, shape, feature_dim)
    first = lax.broadcasted_iota(jnp.int32, shape, head_dim) * HEAD_DIM
    inside = (feature >= first) & (feature < first + HEAD_DIM)
    return jnp.where(inside, 1.0, 0.0).astype(BF16)


def attend_kernel(x_ref, w_ref, q_gain_ref, k_gain_ref, out_ref, q_ref, k_ref, v_ref):
    frames, branch, share, width = x_ref.shape
    tokens = frames * share
    x = x_ref[...].reshape(frames * branch * share, width)
    gather = head_of((width, LANES), 0, 1)
    spread = head_of((LANES, width), 1, 0)

    def per_branch(values, ref):
        values = values.reshape(frames, branch, share, width)
        for b in range(branch):
            ref[b] = values[:, b].reshape(tokens, width).astype(BF16)

    for part, gain_ref, ref in ((0, q_gain_ref, q_ref), (1, k_gain_ref, k_ref)):
        vectors = jnp.dot(
            x, w_ref[:, part * width : (part + 1) * width], preferred_element_type=F32
        )
        square = split_dot(vectors * vectors, gather) * (1.0 / HEAD_DIM)
        factor = split_dot(lax.rsqrt(square + 1e-06), spread)
        per_branch(vectors * factor * gain_ref[...], ref)
    per_branch(jnp.dot(x, w_ref[:, 2 * width :], preferred_element_type=F32), v_ref)

    same = lax.broadcasted_iota(jnp.int32, (share, tokens), 0) == lax.rem(
        lax.broadcasted_iota(jnp.int32, (share, tokens), 1), share
    )
    lane = lax.broadcasted_iota(jnp.int32, (1, 2 * LANES), 1)
    for b in range(branch):
        blocks = {}
        for h in range(HEADS):
            start = h * HEAD_DIM
            low = start // LANES * LANES
            high = min(-(-(start + HEAD_DIM) // LANES) * LANES, width)
            inside = (lane >= start - low) & (lane < start - low + HEAD_DIM)
            inside = inside[:, : high - low]
            query = jnp.where(inside, q_ref[b, :, low:high], jnp.zeros((), BF16))
            scores = lax.dot_general(
                k_ref[b, :, low:high], query, (((1,), (1,)), ((), ())), preferred_element_type=F32
            )
            scores = scores.reshape(frames, share, tokens)
            top = jnp.max(scores, axis=0)
            weights = jnp.exp((scores - top) * HEAD_DIM ** (-0.5))
            total = jnp.sum(weights, axis=0)
            probs = weights * jnp.where(same, 1.0 / total, 0.0)
            probs = probs.reshape(tokens, tokens).astype(BF16)
            mixed = lax.dot_general(
                probs, v_ref[b, :, low:high], (((0,), (0,)), ((), ())), preferred_element_type=F32
            )
            for at in range(low, high, LANES):
                piece = mixed[:, at - low : at - low + LANES]
                if at in blocks:
                    piece = jnp.where(inside[:, at - low : at - low + LANES], piece, blocks[at])
                blocks[at] = piece
            done = [at for at in blocks if at + LANES <= start + HEAD_DIM]
            for at in done:
                block = blocks.pop(at).astype(BF16)
                out_ref[:, b, :, at : at + LANES] = block.reshape(frames, share, LANES)


def attend(x, w_qkv, q_gain, k_gain):
    frames, branch, share, width = x.shape
    tokens = frames * share
    return pl.pallas_call(
        attend_kernel,
        out_shape=jax.ShapeDtypeStruct(x.shape, BF16),
        in_specs=[pl.BlockSpec(memory_space=VMEM)] * 4,
        out_specs=pl.BlockSpec(memory_space=VMEM),
        scratch_shapes=[VMEM((branch, tokens, width), BF16)] * 3,
        name="attend",
    )(x, w_qkv, q_gain.reshape(1, width), k_gain.reshape(1, width))


def project_kernel(step_ref, x_ref, w_ref, mods_ref, residual_ref, out_ref):
    del step_ref
    n, branch, share, width = x_ref.shape
    output = jnp.dot(
        x_ref[...].reshape(n * branch * share, width), w_ref[...], preferred_element_type=F32
    )
    gated = mods_ref[0, 2:3, :] * output
    gated = gated.reshape(n, branch, share, -1)
    for b in range(branch):
        out_ref[b] = residual_ref[b] + gated[:, b].reshape(n * share, -1)


def project(x, w_proj, step_mods, timestep, rows):
    n, branch, share, width = x.shape
    cols = 384
    return pl.pallas_call(
        project_kernel,
        out_shape=jax.ShapeDtypeStruct(rows.shape, F32),
        grid_spec=pltpu.PrefetchScalarGridSpec(
            num_scalar_prefetch=1,
            grid=(width // cols,),
            in_specs=[
                pl.BlockSpec((n, branch, share, width), lambda j, step: (0, 0, 0, 0)),
                pl.BlockSpec((width, cols), lambda j, step: (0, j)),
                pl.BlockSpec((1, 3, cols), lambda j, step: (step[0], 0, j)),
                pl.BlockSpec((branch, n * share, cols), lambda j, step: (0, 0, j)),
            ],
            out_specs=pl.BlockSpec((branch, n * share, cols), lambda j, step: (0, 0, j)),
        ),
        name="project",
    )(timestep, x, w_proj, step_mods, rows)


def body(n, residual, w_qkv, w_proj, q_gain, k_gain, step_mods, timestep):
    rows = residual[:, 0]
    swap = functools.partial(
        lax.all_to_all, axis_name="seq", split_axis=0, concat_axis=0, tiled=True
    )
    modulated = swap(modulate(rows, step_mods, timestep, n))
    attended = swap(attend(modulated, w_qkv, q_gain, k_gain))
    return project(attended, w_proj, step_mods, timestep, rows)[:, None]


def solution(mesh):
    in_specs = (P("groups", "seq", None, None), P(), P(), P(), P(), P(), P("groups"))
    out_specs = P("groups", "seq", None, None)
    step = functools.partial(body, mesh.shape["seq"])
    return jax.shard_map(step, mesh=mesh, in_specs=in_specs, out_specs=out_specs, check_vma=False)
```

time: 79.8 us -> 68.9 us (0.86)
  Pallas kernels: 0 us -> 20.2 us
  matrix products: 19 us -> 0 us
  local copies, waits for them, and re-layouts: 17.7 us -> 4.15 us
  waiting for transfers between devices: 3.65 us -> 14.2 us
  other arithmetic: 8.88 us -> 0 us
    pallas_call x0 -> x3, Pallas kernels: none -> 20.2 us  [the longest x1 13.1 us: attend(): pl.pallas_call(attend_kernel, out_shape=jax.ShapeDtypeStruct(x.shape, BF1...]
    dot_general x3 -> x0, matrix products: 13.2 us -> none  [the longest x1 6.59 us: temporal_heads(): jnp.dot(modulated.reshape(-1, width), w_qkv, preferred_element_type=jnp.f...]
    all_to_all x1, waiting for transfers between devices: 3.65 us -> 14.2 us  [body(): modulated = swap(modulate(rows, step_mods, timestep, n))]
    unnamed x7, local copies, waits for them, and re-layouts: 11.5 us -> 2.97 us
    sub x1 -> x0, matrix products: 5.79 us -> none  [one_block(): weights = jnp.exp(scores - top)]
    reduce_sum x3 -> x0, other arithmetic: 4.1 us -> none  [the longest x1 1.53 us: layer_modulate(): variance = jnp.mean(centred * centred, axis=-1, keepdims=True)]
    convert_element_type x2 -> x0, other arithmetic: 3.83 us -> none  [the longest x1 2.29 us: head_norm(): return (vectors * lax.rsqrt(square + 1e-06) * gain).astype(jnp.bfloat16)]
    another operation x2 -> x0, local copies, waits for them, and re-layouts: 3.48 us -> none  [temporal_heads(): return attended.reshape(branch, frames, patches, width)]
  transfers between devices with their start and end apart: 1 -> 1, of which waited for: 1 -> 1; matrix products, arithmetic and copies ran while one was open for 15% -> 2% of each run, Pallas kernels for 0% -> 0%
where the time goes in v1:
time: 68.9 us; the launch traced here: 68.4 us
  blocking collectives  21.8 us (32%)
  Pallas kernels  20.2 us (29%)
  waiting for transfers between devices  14.2 us (21%)
  starting transfers between devices  7.41 us (11%)
  local copies, waits for them, and re-layouts  4.15 us (6%)
  between operations  0.7 us (1%)
    all_to_all x1, blocking collectives, body(): attended = swap(attend(modulated, w_qkv, q_gain, k_gain))  21.8 us
    all_to_all x1, waiting for transfers between devices, body(): modulated = swap(modulate(rows, step_mods, timestep, n))  14.2 us
    pallas_call x1, Pallas kernels, attend(): pl.pallas_call(attend_kernel, out_shape=jax.ShapeDtypeStruct(x.shape, BF1...  13.1 us
    all_to_all x1, starting transfers between devices, body(): modulated = swap(modulate(rows, step_mods, timestep, n))  7.41 us
    pallas_call x1, Pallas kernels, project(): pl.pallas_call(project_kernel, out_shape=jax.ShapeDtypeStruct(rows.shape,...  4.75 us
    unnamed x7, local copies, waits for them, and re-layouts  2.97 us
    pallas_call x1, Pallas kernels, modulate(): pl.pallas_call(modulate_kernel, out_shape=jax.ShapeDtypeStruct((n, branch...  2.34 us
  transfers between devices with their start and end apart: 1, of which 1 were waited for; matrix products, arithmetic and copies ran while one was open for 2% of the time, Pallas kernels for 0%

profile of v1, /device:TPU:0, one launch (start us, length us, event | category | flops | bytes accessed | tf_op | source)
XLA Modules:
  0.0 68.4 jit_solution(7098510120773438596)
XLA Ops:
  0.0 0.0 copy-start.1
  0.0 0.0 copy-start.2
  0.7 2.1 %copy.8.mods_ref = f32[30,3,1152]{2,1,0:T(4,128)} copy(f32[30,3,1152]{2,0,1:T(8,128)} %param.12) | data formatting | bytes 829440 | tf_op args[5]
  2.8 2.3 %modulate.1 = bf16[16,2,8,1152]{3,2,1,0:T(8,128)(2,1)} custom-call(s32[1]{0:T(128)S(6)} %copy.11.step_ref, f32[2,128,1152]{2,1,0:T(8,128)} %bitcast.4, f32[30,3,1152]{2,1,0:T(4,128)} %copy.8.mods_ref), custom_call_target="tpu_custom_call" | custom-call | tf_op jit(solution)/shard_map/modulate/pallas_call | solution.py:32
  5.2 7.4 %all-to-all-start = ((bf16[16,2,8,1152]{3,2,1,0:T(8,128)(2,1)}), bf16[16,2,8,1152]{3,2,1,0:T(8,128)(2,1)S(1)}, u32[]{:S(2)}, u32[]{:S(2)}) async-start(bf16[16,2,8,1152]{3,2,1,0:T(8,128)(2,1)} %modulate.1), calls=%async_computation | async-start | bytes 1179648 | tf_op jit(solution)/shard_map/all_to_all | solution.py:171
  12.6 0.0 copy-done.1
  12.6 0.6 reshape.6.q_gain_ref
  13.2 0.0 copy-done.2
  13.2 0.6 reshape.7.k_gain_ref
  13.8 14.2 %all-to-all-done.x_ref = bf16[16,2,8,1152]{3,2,1,0:T(8,128)(2,1)S(1)} async-done(((bf16[16,2,8,1152]{3,2,1,0:T(8,128)(2,1)}), bf16[16,2,8,1152]{3,2,1,0:T(8,128)(2,1)S(1)}, u32[]{:S(2)}, u32[]{:S(2)}) %all-to-all-start) | async-done | bytes 589856 | tf_op jit(solution)/shard_map/all_to_all | solution.py:171
  28.0 0.0 copy-start
  28.0 0.8 %copy-done = bf16[16,2,8,1152]{3,2,1,0:T(8,128)(2,1)} copy-done((bf16[16,2,8,1152]{3,2,1,0:T(8,128)(2,1)}, bf16[16,2,8,1152]{3,2,1,0:T(8,128)(2,1)S(1)}, u32[]{:S(2)}) %copy-start) | copy-done | bytes 589848
  28.8 13.1 %attend.1 = bf16[16,2,8,1152]{3,2,1,0:T(8,128)(2,1)} custom-call(bf16[16,2,8,1152]{3,2,1,0:T(8,128)(2,1)} %copy-done, bf16[1152,3456]{1,0:T(8,128)(2,1)} %w_ref.2, f32[1,1152]{1,0:T(1,128)} %reshape.6.q_gain_ref, f32[1,1152]{1,0:T(1,128)} %reshape.7.k_gain_ref), custom_call_target="tpu_custom_call" | custom-call | tf_op jit(solution)/shard_map/attend/pallas_call | solution.py:123
  41.9 21.8 %all_to_all.10.x_ref = bf16[16,2,8,1152]{3,2,1,0:T(8,128)(2,1)} all-to-all(bf16[16,2,8,1152]{3,2,1,0:T(8,128)(2,1)} %attend.1), channel_id=1, replica_groups=mesh['groups'=2,'seq'=16] {'seq'}, dimensions={0} | all-to-all | bytes 1179648 | tf_op jit(solution)/shard_map/all_to_all | solution.py:172
  63.7 4.7 %project.1 = f32[2,128,1152]{2,1,0:T(8,128)} custom-call(s32[1]{0:T(128)S(6)} %copy.11.step_ref, bf16[16,2,8,1152]{3,2,1,0:T(8,128)(2,1)} %all_to_all.10.x_ref, bf16[1152,1152]{1,0:T(8,128)(2,1)} %w_ref.3, f32[30,3,1152]{2,1,0:T(4,128)} %copy.8.mods_ref, f32[2,128,1152]{2,1,0:T(8,128)} %bitcast.5), custom_call_target="tpu_custom_call" | custom-call | tf_op jit(solution)/shard_map/project/pallas_call | solution.py:148
Async XLA Ops:
  0.0 12.6 %copy-start.1 = (f32[1152]{0:T(1024)S(1)}, f32[1152]{0:T(1024)}, u32[]{:S(2)}) copy-start(f32[1152]{0:T(1024)} %param.10) | copy-start | bytes 13828
  0.0 13.2 %copy-start.2 = (f32[1152]{0:T(1024)S(1)}, f32[1152]{0:T(1024)}, u32[]{:S(2)}) copy-start(f32[1152]{0:T(1024)} %param.11) | copy-start | bytes 13828
  5.2 22.8 %all-to-all-start = ((bf16[16,2,8,1152]{3,2,1,0:T(8,128)(2,1)}), bf16[16,2,8,1152]{3,2,1,0:T(8,128)(2,1)S(1)}, u32[]{:S(2)}, u32[]{:S(2)}) async-start(bf16[16,2,8,1152]{3,2,1,0:T(8,128)(2,1)} %modulate.1), calls=%async_computation | async-start | bytes 1179648 | tf_op jit(solution)/shard_map/all_to_all | solution.py:171
  28.0 0.8 %copy-start = (bf16[16,2,8,1152]{3,2,1,0:T(8,128)(2,1)}, bf16[16,2,8,1152]{3,2,1,0:T(8,128)(2,1)S(1)}, u32[]{:S(2)}) copy-start(bf16[16,2,8,1152]{3,2,1,0:T(8,128)(2,1)S(1)} %all-to-all-done.x_ref) | copy-start | bytes 1769476
